TPU v7x, 128 devices: a whole 4x4x4 slice. The times are simulated.
128 devices in a mesh: sta: 16 (over x, y_hi, core), freq: 8 (over y_lo, z).
Axes of the slice: x: 4, y: 4 (y_hi: 2, y_lo: 2; y = y_hi * 2 + y_lo), z: 4, core: 2. Of those that a mesh axis runs over, the one named last changes fastest.
Arguments:
- records: bfloat16 [2048, 256, 512], P('sta', 'freq'), may hold values from -6 to 6
- available: int32 [2048, 256], P('sta', 'freq'), may hold values 0 or 1
Outputs:
- cross_gram: bfloat16 [2, 128, 2048, 2048], P(None, 'freq', 'sta')
All inputs are finite; a program needn't handle non-finite values. No bound on the sum of `available` on one device may be relied on, other than what follows from the above.
Results may differ from a plain program's by a relative error of at most 0.0056.
Values may be sent and summed in bfloat16 or wider, within the bound.
No kernel may reach another device: no remote copies, remote signals or barrier semaphores. Data moves between devices by JAX's collectives and lax.ppermute only.
A program may use at most 192 MiB of HBM per device.

v0:
```python
import jax
import jax.numpy as jnp
from jax import lax
from jax.sharding import PartitionSpec as P

FFT_LEN = 512
BINS = 128
BAND_LO = 16


def spectra_table():
    sample_idx = jnp.arange(FFT_LEN, dtype=jnp.int32)[:, None]
    bin_idx = BAND_LO + jnp.arange(BINS, dtype=jnp.int32)[None, :]
    phase = (sample_idx * bin_idx % FFT_LEN).astype(jnp.float32) * (2.0 * jnp.pi / FFT_LEN)
    return jnp.concatenate([jnp.cos(phase), -jnp.sin(phase)], axis=1)


def gram_block(mine, other):
    count = mine.shape[3]
    both_real = jnp.einsum(
        "fas,fbs->fab", mine[:, 0], other[:, 0], preferred_element_type=jnp.float32
    )
    both_imag = jnp.einsum(
        "fas,fbs->fab", mine[:, 1], other[:, 1], preferred_element_type=jnp.float32
    )
    imag_real = jnp.einsum(
        "fas,fbs->fab", mine[:, 1], other[:, 0], preferred_element_type=jnp.float32
    )
    real_imag = jnp.einsum(
        "fas,fbs->fab", mine[:, 0], other[:, 1], preferred_element_type=jnp.float32
    )
    return jnp.stack([(both_real + both_imag) / count, (imag_real - real_imag) / count]).astype(
        jnp.bfloat16
    )


def shards(records, available):
    stations, segments, samples = records.shape
    sample_pos = jnp.arange(samples, dtype=jnp.float32)
    window_taper = 0.5 - 0.5 * jnp.cos(2.0 * jnp.pi * sample_pos / samples)
    tapered = records.astype(jnp.float32) * window_taper
    spectra = jnp.dot(
        tapered.reshape(stations * segments, samples),
        spectra_table(),
        precision=lax.Precision.HIGHEST,
        preferred_element_type=jnp.float32,
    )
    spectra = spectra.reshape(stations, segments, 2 * BINS)
    real_part = spectra[..., :BINS]
    imag_part = spectra[..., BINS:]
    power = jnp.mean(real_part * real_part + imag_part * imag_part, axis=-1, keepdims=True)
    weight = available.astype(jnp.float32)[..., None] / jnp.sqrt(power + 1e-05)
    whitened = jnp.stack([real_part * weight, imag_part * weight]).astype(jnp.bfloat16)
    whitened = jnp.transpose(whitened, (3, 0, 1, 2))
    panel = lax.all_to_all(whitened, "freq", split_axis=0, concat_axis=3, tiled=True)
    return gram_block(panel, lax.all_gather(panel, "sta", axis=2, tiled=True))


def solution(mesh):
    in_specs = (P("sta", "freq", None), P("sta", "freq"))
    out_specs = P(None, "freq", "sta", None)
    return jax.shard_map(shards, mesh=mesh, in_specs=in_specs, out_specs=out_specs, check_vma=False)
```

profile of v0, /device:TPU:1, one launch (start us, length us, event | category | flops | bytes accessed | tf_op | source)
XLA Modules:
  0.0 333.4 jit_solution(14007002556690948768)
XLA Ops:
  6.5 0.0 all-gather.2.cloned.1.call-start
  6.6 1.1 fusion.18
  7.6 3.4 %convert_multiply_fusion = f32[128,32,512]{2,1,0:T(8,128)S(1)} fusion(bf16[128,32,512]{2,1,0:T(8,128)(2,1)} %param.2, f32[512]{0:T(512)S(1)} %multiply_subtract_fusion), kind=kLoop, calls=%fused_computation.13 | loop fusion | flops 4194304 | bytes 12584960 | tf_op jit(solution)/shard_map/mul | solution.py:41
  11.1 0.0 copy-start.2
  11.1 11.3 %fusion.6 = f32[128,32,256]{2,0,1:T(8,128)S(1)} fusion(f32[128,32,512]{2,1,0:T(8,128)S(1)} %convert_multiply_fusion, f32[512,128]{1,0:T(8,128)S(1)} %get-tuple-element.8, f32[512,128]{1,0:T(8,128)S(1)} %get-tuple-element.7), kind=kOutput, calls=%fused_computation.11 | convolution fusion | flops 6442582016 | bytes 13107200 | tf_op jit(solution)/shard_map/dot_general | solution.py:42
  22.4 0.6 add_reduce_fusion
  23.0 0.0 copy-done.2
  23.0 0.8 fusion.8
  23.9 0.2 maximum_bitcast_fusion
  24.1 2.9 copy.12
  27.0 32.6 %all_to_all.18 = bf16[128,2,128,32]{2,3,1,0:T(8,128)(2,1)S(1)} all-to-all(bf16[128,2,128,32]{2,3,1,0:T(8,128)(2,1)} %copy.12), channel_id=1, replica_groups=mesh['sta'=16,'freq'=8] {'freq'}, dimensions={0} | all-to-all | bytes 4194304 | tf_op jit(solution)/shard_map/all_to_all | solution.py:55
  59.5 0.5 copy.13
  60.0 2.6 copy.14
  62.6 0.0 all-gather.2.cloned.1.call-update
  62.6 0.0 copy-start.1
  62.7 188.9 %all-gather.2.cloned.1.call-done = bf16[16,2,2048,256]{3,2,0,1:T(8,128)(2,1)} async-done(((bf16[16,2,128,256]{3,2,0,1:T(8,128)(2,1)}), bf16[16,2,2048,256]{3,2,0,1:T(8,128)(2,1)}) %all-gather.2.cloned.1.call-update) | async-done | bytes 33554448 | tf_op jit(solution)/shard_map/all_gather | solution.py:56
  251.6 12.8 %fusion = f32[16,128,2048]{2,1,0:T(8,128)} fusion(bf16[16,2,2048,256]{3,2,0,1:T(8,128)(2,1)} %all-gather.2.cloned.1.call-done, bf16[16,2,128,256]{3,2,0,1:T(8,128)(2,1)} %copy.14), kind=kOutput, calls=%fused_computation.5 | convolution fusion | flops 2147483648 | bytes 34603008 | tf_op jit(solution)/shard_map/fas,fbs->fab/dot_general | solution.py:26
  264.4 0.0 copy-done.1
  264.4 12.3 %fusion.1 = f32[16,128,2048]{2,1,0:T(8,128)} fusion(bf16[16,2,2048,256]{3,2,0,1:T(8,128)(2,1)} %all-gather.2.cloned.1.call-done, bf16[16,2,128,256]{3,2,0,1:T(8,128)(2,1)S(1)} %copy-done.1), kind=kOutput, calls=%fused_computation.6 | convolution fusion | flops 2147483648 | bytes 34603008 | tf_op jit(solution)/shard_map/fas,fbs->fab/dot_general | solution.py:20
  276.6 0.0 copy-start
  276.6 15.5 %fusion.5 = bf16[1,16,128,2048]{3,2,1,0:T(8,128)(2,1)} fusion(f32[16,128,2048]{2,1,0:T(8,128)} %fusion, bf16[16,2,2048,256]{3,2,0,1:T(8,128)(2,1)} %all-gather.2.cloned.1.call-done, bf16[16,2,128,256]{3,2,0,1:T(8,128)(2,1)S(1)} %copy-done.1), kind=kOutput, calls=%fused_computation.10 | convolution fusion | flops 2160066560 | bytes 42991616 | tf_op jit(solution)/shard_map/fas,fbs->fab/dot_general | solution.py:29
  292.1 2.9 copy-done
  295.1 17.7 %fusion.4 = bf16[1,16,128,2048]{3,2,1,0:T(8,128)(2,1)} fusion(f32[16,128,2048]{2,1,0:T(8,128)S(1)} %copy-done, bf16[16,2,2048,256]{3,2,0,1:T(8,128)(2,1)} %all-gather.2.cloned.1.call-done, bf16[16,2,128,256]{3,2,0,1:T(8,128)(2,1)S(1)} %copy-done.1), kind=kOutput, calls=%fused_computation.9 | convolution fusion | flops 2160066560 | bytes 42991616 | tf_op jit(solution)/shard_map/fas,fbs->fab/dot_general | solution.py:23
  312.8 13.8 %pad_maximum_fusion = bf16[2,16,128,2048]{3,2,1,0:T(8,128)(2,1)} fusion(bf16[1,16,128,2048]{3,2,1,0:T(8,128)(2,1)} %fusion.5, bf16[1,16,128,2048]{3,2,1,0:T(8,128)(2,1)} %fusion.4), kind=kLoop, calls=%fused_computation.2 | loop fusion | flops 8388608 | bytes 33554432 | tf_op jit(solution)/shard_map/stack | solution.py:32
  (3 shorter events, 0.1 us)
Async XLA Ops:
  6.5 245.0 %all-gather.2.cloned.1.call-start = ((), (), s32[]{:S(2)}) async-start(), calls=%async_computation.1 | async-start | bytes 35651584 | tf_op jit(solution)/shard_map/all_gather | solution.py:56
  11.1 11.9 %copy-start.2 = (s32[128,32]{0,1:T(8,128)S(1)}, s32[128,32]{0,1:T(8,128)}, u32[]{:S(2)}) copy-start(s32[128,32]{0,1:T(8,128)} %param.3) | copy-start | bytes 49156
  62.6 201.7 %copy-start.1 = (bf16[16,2,128,256]{3,2,0,1:T(8,128)(2,1)S(1)}, bf16[16,2,128,256]{3,2,0,1:T(8,128)(2,1)}, u32[]{:S(2)}) copy-start(bf16[16,2,128,256]{3,2,0,1:T(8,128)(2,1)} %copy.14) | copy-start | bytes 6291460
  276.6 18.4 %copy-start = (f32[16,128,2048]{2,1,0:T(8,128)S(1)}, f32[16,128,2048]{2,1,0:T(8,128)}, u32[]{:S(2)}) copy-start(f32[16,128,2048]{2,1,0:T(8,128)} %fusion.1) | copy-start | bytes 50331652
Sparse Core Ops, SparseCore 0:
  62.8 188.7 all-gather.1
where the time goes:
time: 334 us; the launch traced here: 333 us
  waiting for transfers between devices  189 us (57%)
  matrix products  69.5 us (21%)
  blocking collectives  32.6 us (10%)
  other arithmetic  20 us (6%)
  between operations  13.5 us (4%)
  local copies, waits for them, and re-layouts  8.93 us (3%)
    all_gather x1, waiting for transfers between devices, shards(): return gram_block(panel, lax.all_gather(panel, 'sta', axis=2, tiled=True))  189 us
    all_to_all x1, blocking collectives, shards(): lax.all_to_all(whitened, 'freq', split_axis=0, concat_axis=3, tiled=True)  32.6 us
    dot_general x1, matrix products, gram_block(): jnp.einsum('fas,fbs->fab', mine[:, 1], other[:, 1], preferred_element_typ...  17.7 us
    dot_general x1, matrix products, gram_block(): jnp.einsum('fas,fbs->fab', mine[:, 0], other[:, 1], preferred_element_typ...  15.5 us
    another operation x1, other arithmetic, gram_block(): jnp.stack([(both_real + both_imag) / count, (imag_real - real_imag) / cou...  13.8 us
    dot_general x1, matrix products, gram_block(): jnp.einsum('fas,fbs->fab', mine[:, 1], other[:, 0], preferred_element_typ...  12.8 us
    dot_general x1, matrix products, gram_block(): jnp.einsum('fas,fbs->fab', mine[:, 0], other[:, 0], preferred_element_typ...  12.3 us
    dot_general x1, matrix products, shards(): jnp.dot(tapered.reshape(stations * segments, samples), spectra_table(), p...  11.3 us
  transfers between devices with their start and end apart: 1, of which 1 were waited for; matrix products, arithmetic and copies ran while one was open for 0% of the time, Pallas kernels for 0%

commit v1 on v0

--- a/solution.py
+++ b/solution.py
@@ -53,7 +53,13 @@
     whitened = jnp.stack([real_part * weight, imag_part * weight]).astype(jnp.bfloat16)
     whitened = jnp.transpose(whitened, (3, 0, 1, 2))
     panel = lax.all_to_all(whitened, "freq", split_axis=0, concat_axis=3, tiled=True)
-    return gram_block(panel, lax.all_gather(panel, "sta", axis=2, tiled=True))
+    return gram_block(
+        panel,
+        jnp.concatenate(
+            lax.all_to_all(jnp.stack([panel for _ in range(lax.axis_size("sta"))]), "sta", 0, 0),
+            axis=2,
+        ),
+    )
 
 
 def solution(mesh):

time: 334 us -> 542 us (1.62)
  blocking collectives: 32.6 us -> 408 us
  waiting for transfers between devices: 189 us -> 0 us
  local copies, waits for them, and re-layouts: 8.93 us -> 44.3 us
  between operations: 13.5 us -> 0.08 us
    all_to_all x0 -> x1, blocking collectives: none -> 375 us  [shards(): lax.all_to_all(jnp.stack([panel for _ in range(lax.axis_size('sta'))]), '...]
    all_gather x1 -> x0, waiting for transfers between devices: 189 us -> none  [shards(): return gram_block(panel, lax.all_gather(panel, 'sta', axis=2, tiled=True))]
    reshape x0 -> x1, local copies, waits for them, and re-layouts: none -> 22.7 us  [shards(): jnp.concatenate(lax.all_to_all(jnp.stack([panel for _ in range(lax.axis_s...]
    another operation x0 -> x1, local copies, waits for them, and re-layouts: none -> 11.1 us  [shards(): jnp.stack([panel for _ in range(lax.axis_size('sta'))])]
  transfers between devices with their start and end apart: 1 -> 0, of which waited for: 1 -> 0; matrix products, arithmetic and copies ran while one was open for 0% -> 0% of each run, Pallas kernels for 0% -> 0%
where the time goes in v1:
time: 542 us; the launch traced here: 541 us
  blocking collectives  408 us (75%)
  matrix products  69.1 us (13%)
  local copies, waits for them, and re-layouts  44.3 us (8%)
  other arithmetic  20 us (4%)
    all_to_all x1, blocking collectives, shards(): lax.all_to_all(jnp.stack([panel for _ in range(lax.axis_size('sta'))]), '...  375 us
    all_to_all x1, blocking collectives, shards(): lax.all_to_all(whitened, 'freq', split_axis=0, concat_axis=3, tiled=True)  32.6 us
    reshape x1, local copies, waits for them, and re-layouts, shards(): jnp.concatenate(lax.all_to_all(jnp.stack([panel for _ in range(lax.axis_s...  22.7 us
    dot_general x1, matrix products, gram_block(): jnp.einsum('fas,fbs->fab', mine[:, 1], other[:, 1], preferred_element_typ...  17.6 us
    dot_general x1, matrix products, gram_block(): jnp.einsum('fas,fbs->fab', mine[:, 0], other[:, 1], preferred_element_typ...  15.5 us
    another operation x1, other arithmetic, gram_block(): jnp.stack([(both_real + both_imag) / count, (imag_real - real_imag) / cou...  13.8 us
    dot_general x1, matrix products, gram_block(): jnp.einsum('fas,fbs->fab', mine[:, 1], other[:, 0], preferred_element_typ...  12.5 us
    dot_general x1, matrix products, gram_block(): jnp.einsum('fas,fbs->fab', mine[:, 0], other[:, 0], preferred_element_typ...  12.3 us

profile of v1, /device:TPU:1, one launch (start us, length us, event | category | flops | bytes accessed | tf_op | source)
XLA Modules:
  0.0 541.1 jit_solution(5550109565792005117)
XLA Ops:
  0.1 1.1 fusion.18
  1.1 3.4 convert_multiply_fusion
  4.5 0.0 copy-start.1
  4.6 11.3 %fusion.6 = f32[128,32,256]{2,0,1:T(8,128)S(1)} fusion(f32[128,32,512]{2,1,0:T(8,128)S(1)} %convert_multiply_fusion, f32[512,128]{1,0:T(8,128)S(1)} %get-tuple-element.8, f32[512,128]{1,0:T(8,128)S(1)} %get-tuple-element.7), kind=kOutput, calls=%fused_computation.11 | convolution fusion | flops 6442582016 | bytes 13107200 | tf_op jit(solution)/shard_map/dot_general | solution.py:42
  15.9 0.6 add_reduce_fusion
  16.5 0.0 copy-done.1
  16.5 0.8 fusion.8
  17.3 0.2 maximum_bitcast_fusion
  17.5 2.9 copy.12
  20.4 32.6 %all_to_all.23 = bf16[128,2,128,32]{2,3,1,0:T(8,128)(2,1)S(1)} all-to-all(bf16[128,2,128,32]{2,3,1,0:T(8,128)(2,1)} %copy.12), channel_id=1, replica_groups=mesh['sta'=16,'freq'=8] {'freq'}, dimensions={0} | all-to-all | bytes 4194304 | tf_op jit(solution)/shard_map/all_to_all | solution.py:55
  53.0 1.8 copy.13
  54.8 2.9 copy.14
  57.7 11.1 %stack.46 = bf16[16,16,2,128,256]{4,3,1,2,0:T(8,128)(2,1)} broadcast(bf16[16,2,128,256]{3,2,0,1:T(8,128)(2,1)S(1)} %copy.14), dimensions={1,2,3,4} | broadcast | bytes 35651584 | tf_op jit(solution)/shard_map/stack | solution.py:59
  68.7 375.1 %all_to_all.24 = bf16[16,16,2,128,256]{4,3,1,2,0:T(8,128)(2,1)} all-to-all(bf16[16,16,2,128,256]{4,3,1,2,0:T(8,128)(2,1)} %stack.46), channel_id=1, replica_groups=mesh['sta'=16,'freq'=8] {'sta'}, dimensions={0} | all-to-all | bytes 67108864 | tf_op jit(solution)/shard_map/all_to_all | solution.py:59
  443.8 22.7 %copy.16 = bf16[16,2,16,128,256]{4,3,2,0,1:T(8,128)(2,1)} copy(bf16[16,2,16,128,256]{4,3,0,1,2:T(8,128)(2,1)} %bitcast.43) | data formatting | bytes 67108864 | tf_op jit(solution)/shard_map/reshape | solution.py:58
  466.5 12.5 %fusion = f32[16,128,2048]{2,1,0:T(8,128)} fusion(bf16[16,2,2048,256]{3,2,0,1:T(8,128)(2,1)} %bitcast.39, bf16[16,2,128,256]{3,2,0,1:T(8,128)(2,1)S(1)} %copy.14), kind=kOutput, calls=%fused_computation.5 | convolution fusion | flops 2147483648 | bytes 34603008 | tf_op jit(solution)/shard_map/fas,fbs->fab/dot_general | solution.py:26
  479.0 12.3 %fusion.1 = f32[16,128,2048]{2,1,0:T(8,128)} fusion(bf16[16,2,2048,256]{3,2,0,1:T(8,128)(2,1)} %bitcast.40, bf16[16,2,128,256]{3,2,0,1:T(8,128)(2,1)S(1)} %copy.14), kind=kOutput, calls=%fused_computation.6 | convolution fusion | flops 2147483648 | bytes 34603008 | tf_op jit(solution)/shard_map/fas,fbs->fab/dot_general | solution.py:20
  491.3 0.0 copy-start
  491.3 15.5 %fusion.5 = bf16[1,16,128,2048]{3,2,1,0:T(8,128)(2,1)} fusion(f32[16,128,2048]{2,1,0:T(8,128)} %fusion, bf16[16,2,2048,256]{3,2,0,1:T(8,128)(2,1)} %bitcast.41, bf16[16,2,128,256]{3,2,0,1:T(8,128)(2,1)S(1)} %copy.14), kind=kOutput, calls=%fused_computation.10 | convolution fusion | flops 2160066560 | bytes 42991616 | tf_op jit(solution)/shard_map/fas,fbs->fab/dot_general | solution.py:29
  506.7 2.9 copy-done
  509.7 17.6 %fusion.4 = bf16[1,16,128,2048]{3,2,1,0:T(8,128)(2,1)} fusion(f32[16,128,2048]{2,1,0:T(8,128)S(1)} %copy-done, bf16[16,2,2048,256]{3,2,0,1:T(8,128)(2,1)} %bitcast.42, bf16[16,2,128,256]{3,2,0,1:T(8,128)(2,1)S(1)} %copy.14), kind=kOutput, calls=%fused_computation.9 | convolution fusion | flops 2160066560 | bytes 42991616 | tf_op jit(solution)/shard_map/fas,fbs->fab/dot_general | solution.py:23
  527.3 13.8 %pad_maximum_fusion = bf16[2,16,128,2048]{3,2,1,0:T(8,128)(2,1)} fusion(bf16[1,16,128,2048]{3,2,1,0:T(8,128)(2,1)} %fusion.5, bf16[1,16,128,2048]{3,2,1,0:T(8,128)(2,1)} %fusion.4), kind=kLoop, calls=%fused_computation.2 | loop fusion | flops 8388608 | bytes 33554432 | tf_op jit(solution)/shard_map/stack | solution.py:32
  (3 shorter events, 0.1 us)
Async XLA Ops:
  4.5 11.9 %copy-start.1 = (s32[128,32]{0,1:T(8,128)S(1)}, s32[128,32]{0,1:T(8,128)}, u32[]{:S(2)}) copy-start(s32[128,32]{0,1:T(8,128)} %param.3) | copy-start | bytes 49156
  491.3 18.4 %copy-start = (f32[16,128,2048]{2,1,0:T(8,128)S(1)}, f32[16,128,2048]{2,1,0:T(8,128)}, u32[]{:S(2)}) copy-start(f32[16,128,2048]{2,1,0:T(8,128)} %fusion.1) | copy-start | bytes 50331652
